TPU v7x, 512 devices: a whole 4x8x8 slice. The times are simulated.
512 devices in a mesh: pipe: 8 (over y_hi, core), ctx: 16 (over z, y_lo), dp: 4 (over x).
Axes of the slice: x: 4, y: 8 (y_hi: 4, y_lo: 2; y = y_hi * 2 + y_lo), z: 8, core: 2. Of those that a mesh axis runs over, the one named last changes fastest.
Arguments:
- state: bfloat16 [8, 4, 2048, 1024], P('pipe', 'dp', 'ctx'), may hold values from -36 to 36
- weights: bfloat16 [2, 8, 1024, 256], P(None, 'pipe'), may hold values from -0.1875 to 0.1875
- out_grad: bfloat16 [2, 8, 4, 2048, 1024], P(None, 'pipe', 'dp', 'ctx'), may hold values from -0.59765625 to 0.59765625
- start_span: int32 [8, 4], P(None, 'dp'), may hold values from 0 to 1
- block_order: int32 [32], replicated, may hold values from 0 to 31, each once
Outputs:
- state_out: bfloat16 [8, 4, 2048, 1024], P('pipe', 'dp', 'ctx')
- weight_grads: float32 [2, 8, 1024, 256], P(None, 'pipe')
All inputs are finite; a program needn't handle non-finite values.
Results may differ from a plain program's by a relative error of at most 0.012.
Values may be sent and summed in bfloat16 or wider, within the bound.
No kernel may reach another device: no remote copies, remote signals or barrier semaphores. Data moves between devices by JAX's collectives and lax.ppermute only.
A program may use at most 64 MiB of HBM per device.

v0:
```python
import math
import jax
import jax.numpy as jnp
from jax import lax
from jax.sharding import PartitionSpec as P

EPS = 1e-05


def from_behind(block, axis, distance):
    devices = range(lax.axis_size(axis))
    route = [((i - distance) % len(devices), i) for i in devices]
    return lax.ppermute(block, axis, route)


def rms_scale(values):
    return lax.rsqrt(jnp.mean(values * values, axis=-1, keepdims=True) + EPS)


def token_positions(block_order, seq_total):
    half_count = block_order.shape[0]
    half_len = seq_total // half_count
    row_ids = jnp.arange(seq_total, dtype=jnp.int32)
    selected = (row_ids // half_len)[:, None] == jnp.arange(half_count, dtype=jnp.int32)[None, :]
    block_ids = jnp.sum(jnp.where(selected, block_order[None, :], 0), axis=1)
    return block_ids * half_len + row_ids % half_len


def shards(state, weights, out_grad, start_span, block_order):
    tok_rows = state.shape[2]
    feat_width = state.shape[3]
    head_dim = weights.shape[3] // 2
    head_count = feat_width // head_dim
    group_size = math.gcd(head_count, 4)
    group_count = head_count // group_size
    span_count = weights.shape[0]
    section_count = lax.axis_size("pipe")
    seq_total = tok_rows * lax.axis_size("ctx")
    score_scale = 1.0 / math.sqrt(head_dim)
    all_positions = token_positions(block_order, seq_total)
    own_positions = lax.dynamic_slice_in_dim(
        all_positions, lax.axis_index("ctx") * tok_rows, tok_rows
    )
    causal = all_positions[None, :] <= own_positions[:, None]
    section_index = lax.axis_index("pipe")
    carried = state[0, 0]
    start_column = start_span[:, 0]
    weight_grads = jnp.zeros((span_count, feat_width, 2 * head_dim), jnp.float32)
    for tick_index in range(out_grad.shape[0]):
        anchor = (section_index - tick_index) % section_count
        first_span = jnp.sum(
            jnp.where(jnp.arange(section_count, dtype=jnp.int32) == anchor, start_column, 0)
        )
        span_index = (first_span + (anchor + tick_index) // section_count) % 2
        weight = lax.dynamic_index_in_dim(weights[:, 0], span_index, 0, keepdims=False)
        widened = carried.astype(jnp.float32)
        normed = (widened * rms_scale(widened)).astype(jnp.bfloat16)
        split_heads = widened.reshape(tok_rows, head_count, head_dim)
        queries = (split_heads * rms_scale(split_heads)).astype(jnp.bfloat16)
        projected = jnp.dot(normed, weight, preferred_element_type=jnp.float32)
        key_raw = projected[:, :head_dim]
        key_scale = rms_scale(key_raw)
        key_unit = key_raw * key_scale
        own_rows = jnp.concatenate([key_unit, projected[:, head_dim:]], axis=1).astype(jnp.bfloat16)
        gathered = lax.all_gather(own_rows, "ctx", axis=0, tiled=True)
        key_rows = gathered[:, :head_dim]
        value_rows = gathered[:, head_dim:]
        query_groups = queries.reshape(tok_rows, group_count, group_size, head_dim).transpose(
            1, 0, 2, 3
        )

        def forward_group(query_part):
            scores = (
                jnp.einsum("qhd,kd->hqk", query_part, key_rows, preferred_element_type=jnp.float32)
                * score_scale
            )
            exponent = jnp.where(causal[None], jnp.exp(scores), 0.0)
            total_weight = jnp.sum(exponent, axis=-1, keepdims=True)
            probs = (exponent / total_weight).astype(jnp.bfloat16)
            attended = jnp.einsum(
                "hqk,kd->qhd", probs, value_rows, preferred_element_type=jnp.float32
            )
            return (probs, attended)

        probs, attended = lax.map(forward_group, query_groups)
        output = attended.transpose(1, 0, 2, 3).reshape(tok_rows, feat_width)
        updated = (widened + output * rms_scale(output)).astype(jnp.bfloat16)
        carried = from_behind(updated, "pipe", 1)
        upstream = out_grad[tick_index, 0, 0]
        upstream_groups = upstream.reshape(tok_rows, group_count, group_size, head_dim).transpose(
            1, 0, 2, 3
        )
        row_delta = jnp.sum(upstream_groups.astype(jnp.float32) * attended, axis=-1).transpose(
            0, 2, 1
        )
        key_grad = jnp.zeros((tok_rows * lax.axis_size("ctx"), head_dim), jnp.float32)
        value_grad = jnp.zeros((tok_rows * lax.axis_size("ctx"), head_dim), jnp.float32)
        for head_block in range(group_count):
            prob_part = probs[head_block]
            value_grad = value_grad + jnp.einsum(
                "hqk,qhd->kd",
                prob_part,
                upstream_groups[head_block],
                preferred_element_type=jnp.float32,
            )
            prob_grad = jnp.einsum(
                "qhd,kd->hqk",
                upstream_groups[head_block],
                value_rows,
                preferred_element_type=jnp.float32,
            )
            score_grad = (
                prob_part.astype(jnp.float32)
                * (prob_grad - row_delta[head_block][..., None])
                * score_scale
            ).astype(jnp.bfloat16)
            key_grad = key_grad + jnp.einsum(
                "hqk,qhd->kd",
                score_grad,
                query_groups[head_block],
                preferred_element_type=jnp.float32,
            )
        key_sums = lax.psum_scatter(
            jnp.concatenate([key_grad, value_grad], axis=1).astype(jnp.bfloat16),
            "ctx",
            scatter_dimension=0,
            tiled=True,
        ).astype(jnp.float32)
        key_delta = key_sums[:, :head_dim]
        key_back = key_scale * (
            key_delta - key_unit * jnp.mean(key_delta * key_unit, axis=-1, keepdims=True)
        )
        grad_rows = jnp.concatenate([key_back, key_sums[:, head_dim:]], axis=1).astype(jnp.bfloat16)
        local_grad = lax.dot_general(
            normed, grad_rows, (((0,), (0,)), ((), ())), preferred_element_type=jnp.float32
        )
        span_mask = (jnp.arange(span_count, dtype=jnp.int32) == span_index).astype(jnp.float32)[
            :, None, None
        ]
        masked_grad = span_mask * local_grad
        weight_grads = weight_grads + masked_grad
    weight_grads = lax.psum(weight_grads, ("ctx", "dp"))
    return (carried[None, None], weight_grads[:, None])


def solution(mesh):
    return jax.shard_map(
        shards,
        mesh=mesh,
        in_specs=(
            P("pipe", "dp", "ctx", None),
            P(None, "pipe", None, None),
            P(None, "pipe", "dp", "ctx", None),
            P(None, "dp"),
            P(),
        ),
        out_specs=(P("pipe", "dp", "ctx", None), P(None, "pipe", None, None)),
        check_vma=False,
    )
```

profile of v0, /device:TPU:16, one launch (start us, length us, event | category | flops | bytes accessed | tf_op | source)
XLA Modules:
  0.0 990.2 jit_solution(8186478735265335391)
XLA Ops:
  16.2 74.4 %all-gather.3.cloned.1.call-done = bf16[2048,256]{1,0:T(8,128)(2,1)} async-done(((bf16[128,256]{1,0:T(8,128)(2,1)}), bf16[2048,256]{1,0:T(8,128)(2,1)}) %all-gather.3.cloned.1.call-update) | async-done | bytes 1048592 | tf_op jit(solution)/shard_map/all_gather | solution.py:65
  92.7 2.5 broadcast.232.clone2
  95.2 22.0 %while.26 = (s32[]{:T(128)}, bf16[2,4,128,2048]{2,3,1,0:T(8,128)(2,1)}, f32[2,128,4,128]{3,1,2,0:T(8,128)}, bf16[2,128,4,128]{1,3,2,0:T(8,128)(2,1)}, bf16[2048,...) while((s32[]{:T(128)}, ...), condition=%wide.region_7.8_spmd.clone, body=%wide.region_5.7_spmd.clone.sunk | while | flops 548666880 | bytes 33962720 | solution.py:85
  95.4 2.3 bitcast_reduce_fusion.4
  100.5 2.5 copy.225
  103.0 3.2 constant_dynamic-update-slice_fusion.4
  106.4 2.3 bitcast_reduce_fusion.4
  111.5 2.5 copy.225
  114.0 3.1 constant_dynamic-update-slice_fusion.4
  122.8 6.8 collective-permute-done
  134.4 2.3 convolution_bitcast_fusion.6
  136.7 2.3 fusion.38
  139.0 4.0 convolution_bitcast_fusion.8
  143.1 3.4 fusion.39
  149.1 56.5 %all-gather.5.cloned.1.call-done = bf16[2048,256]{1,0:T(8,128)(2,1)} async-done(((bf16[128,256]{1,0:T(8,128)(2,1)}), bf16[2048,256]{1,0:T(8,128)(2,1)}) %all-gather.5.cloned.1.call-update) | async-done | bytes 1048592 | tf_op jit(solution)/shard_map/all_gather | solution.py:65
  207.7 2.5 broadcast.232.clone
  210.1 22.0 %while.27 = (s32[]{:T(128)}, bf16[2,4,128,2048]{2,3,1,0:T(8,128)(2,1)}, f32[2,128,4,128]{3,1,2,0:T(8,128)}, bf16[2,128,4,128]{1,3,2,0:T(8,128)(2,1)}, bf16[2048,...) while((s32[]{:T(128)}, ...), condition=%wide.region_15.16_spmd.clone, body=%wide.region_13.15_spmd.clone.sunk | while | flops 548666880 | bytes 33962720 | solution.py:85
  210.4 2.3 bitcast_reduce_fusion.5
  215.5 2.5 copy.226
  218.0 3.2 constant_dynamic-update-slice_fusion.5
  221.4 2.3 bitcast_reduce_fusion.5
  226.5 2.5 copy.226
  229.0 3.1 constant_dynamic-update-slice_fusion.5
  233.6 2.3 convolution_bitcast_fusion.2
  235.9 2.3 fusion.36
  238.2 3.9 convolution_bitcast_fusion.4
  242.1 4.0 fusion.37
  248.4 35.8 %reduce-scatter.3.cloned.1.call-done = bf16[128,256]{1,0:T(8,128)(2,1)} async-done(((bf16[2048,256]{1,0:T(8,128)(2,1)}), bf16[128,256]{1,0:T(8,128)(2,1)}) %reduce-scatter.3.cloned.1.call-update) | async-done | bytes 65552 | tf_op jit(solution)/shard_map/reduce_scatter | solution.py:123
  287.2 73.8 %reduce-scatter.5.cloned.1.call-done = bf16[128,256]{1,0:T(8,128)(2,1)} async-done(((bf16[2048,256]{1,0:T(8,128)(2,1)}), bf16[128,256]{1,0:T(8,128)(2,1)}) %reduce-scatter.5.cloned.1.call-update) | async-done | bytes 65552 | tf_op jit(solution)/shard_map/reduce_scatter | solution.py:123
  370.5 7.2 collective-permute-done.1
  377.7 602.2 %all-reduce.2.cloned.1.call-done = f32[2,1,1024,256]{3,2,1,0:T(8,128)} async-done(((f32[2,1,1024,256]{3,2,1,0:T(8,128)}), f32[2,1,1024,256]{3,2,1,0:T(8,128)}) %all-reduce.2.cloned.1.call-update) | async-done | bytes 2097168 | tf_op jit(solution)/shard_map/psum | solution.py:142
  980.6 3.0 copy.256
  (160 shorter events, 53.3 us)
Async XLA Ops:
  7.2 3.3 copy-start
  7.2 8.0 copy-start.23
  7.2 83.4 %all-gather.3.cloned.1.call-start = ((), (), s32[]{:S(2)}) async-start(), calls=%async_computation.2 | async-start | bytes 1114112 | tf_op jit(solution)/shard_map/all_gather | solution.py:65
  12.6 192.9 %all-gather.5.cloned.1.call-start = ((), (), s32[]{:S(2)}) async-start(), calls=%async_computation.3 | async-start | bytes 1114112 | tf_op jit(solution)/shard_map/all_gather | solution.py:65
  95.2 24.8 %copy-start.1 = (bf16[1,1,128,1024]{3,2,1,0:T(8,128)(2,1)S(1)}, bf16[1,1,128,1024]{3,2,1,0:T(8,128)(2,1)}, u32[]{:S(2)}) copy-start(bf16[1,1,128,1024]{3,2,1,0:T(8,128)(2,1)} %param.9) | copy-start | bytes 786436
  95.2 2.6 copy-start.15
  103.0 3.2 copy-start.14
  103.0 3.2 copy-start.16
  106.2 2.6 copy-start.15
  114.0 3.1 copy-start.14
  114.0 3.1 copy-start.16
  117.1 14.0 %copy-start.8 = (bf16[2,1,1,128,1024]{4,3,2,1,0:T(8,128)(2,1)S(1)}, bf16[2,1,1,128,1024]{4,3,2,1,0:T(8,128)(2,1)}, u32[]{:S(2)}) copy-start(bf16[2,1,1,128,1024]{4,3,2,1,0:T(8,128)(2,1)} %param.11) | copy-start | bytes 1572868
  120.1 9.4 collective-permute-start
  129.6 18.6 %copy-start.2 = (bf16[128,1024]{1,0:T(8,128)(2,1)}, bf16[128,1024]{1,0:T(8,128)(2,1)S(1)}, u32[]{:S(2)}) copy-start(bf16[128,1024]{1,0:T(8,128)(2,1)S(1)} %collective-permute-done) | copy-start | bytes 786436
  130.0 4.4 copy-start.5
  131.1 153.1 %reduce-scatter.3.cloned.1.call-start = ((), (), s32[]{:S(2)}) async-start(), calls=%async_computation.4 | async-start | bytes 1114112 | tf_op jit(solution)/shard_map/reduce_scatter | solution.py:123
  147.6 213.4 %reduce-scatter.5.cloned.1.call-start = ((), (), s32[]{:S(2)}) async-start(), calls=%async_computation.5 | async-start | bytes 1114112 | tf_op jit(solution)/shard_map/reduce_scatter | solution.py:123
  210.1 2.6 copy-start.11
  218.0 3.2 copy-start.10
  218.0 3.2 copy-start.12
  221.2 2.6 copy-start.11
  229.0 3.1 copy-start.10
  229.0 3.1 copy-start.12
  232.1 3.8 copy-start.4
  232.1 6.1 copy-start.7
  242.1 44.6 %copy-start.20 = (f32[128]{0:T(128)S(1)}, f32[128]{0:T(128)}, u32[]{:S(2)}) copy-start(f32[128]{0:T(128)} %copy-done.19) | copy-start | bytes 1540
  246.1 114.8 %copy-start.6 = (f32[128,256]{1,0:T(8,128)S(1)}, f32[128,256]{1,0:T(8,128)}, u32[]{:S(2)}) copy-start(f32[128,256]{1,0:T(8,128)} %copy-done.5) | copy-start | bytes 393220
  246.1 114.8 %copy-start.18 = (f32[128]{0:T(128)S(1)}, f32[128]{0:T(128)}, u32[]{:S(2)}) copy-start(f32[128]{0:T(128)} %copy-done.17) | copy-start | bytes 1540
  246.1 117.4 %copy-start.3 = (bf16[128,1024]{1,0:T(8,128)(2,1)S(1)}, bf16[128,1024]{1,0:T(8,128)(2,1)}, u32[]{:S(2)}) copy-start(bf16[128,1024]{1,0:T(8,128)(2,1)} %copy-done.2) | copy-start | bytes 786436
  246.1 117.4 %copy-start.22 = (f32[128]{0:T(128)S(1)}, f32[128]{0:T(128)}, u32[]{:S(2)}) copy-start(f32[128]{0:T(128)} %copy-done.21) | copy-start | bytes 1540
  248.4 731.6 %all-reduce.2.cloned.1.call-start = ((), (), s32[]{:S(2)}) async-start(), calls=%async_computation.6 | async-start | bytes 4194304 | tf_op jit(solution)/shard_map/psum | solution.py:142
  368.5 9.2 collective-permute-start.1
  (7 other events, 13.1 us)
Sparse Core Ops, SparseCore 0:
  12.8 77.7 all-gather.2
  131.2 74.3 all-gather.4
  208.4 75.7 reduce-scatter.2
  287.7 73.2 reduce-scatter.4
  365.7 614.1 all-reduce.1
where the time goes:
time: 992 us; the launch traced here: 990 us
  waiting for transfers between devices  857 us (86%)
  local copies, waits for them, and re-layouts  44.1 us (4%)
  matrix products  43.5 us (4%)
  other arithmetic  25.8 us (3%)
  between operations  15.7 us (2%)
    psum x1, waiting for transfers between devices, shards(): weight_grads = lax.psum(weight_grads, ('ctx', 'dp'))  602 us
    all_gather x2, waiting for transfers between devices, shards(): gathered = lax.all_gather(own_rows, 'ctx', axis=0, tiled=True)  131 us
    reduce_scatter x2, waiting for transfers between devices, shards(): lax.psum_scatter(jnp.concatenate([key_grad, value_grad], axis=1).astype(j...  110 us
    dynamic_update_slice x8, local copies, waits for them, and re-layouts, shards(): probs, attended = lax.map(forward_group, query_groups)  22.5 us
  transfers between devices with their start and end apart: 7, of which 7 were waited for; matrix products, arithmetic and copies ran while one was open for 7% of the time, Pallas kernels for 0%

commit v1 on v0

--- a/solution.py
+++ b/solution.py
@@ -139,7 +139,7 @@
         ]
         masked_grad = span_mask * local_grad
         weight_grads = weight_grads + masked_grad
-    weight_grads = lax.psum(weight_grads, ("ctx", "dp"))
+    weight_grads = lax.psum(lax.psum(weight_grads, "ctx"), "dp")
     return (carried[None, None], weight_grads[:, None])
 
 

time: 992 us -> 603 us (0.61)
  the two profiles are of different devices: /device:TPU:16 before, /device:TPU:1 now
where the time goes in v1:
time: 603 us; the launch traced here: 602 us
  waiting for transfers between devices  444 us (74%)
  local copies, waits for them, and re-layouts  44.1 us (7%)
  matrix products  43.5 us (7%)
  starting transfers between devices  28.5 us (5%)
  other arithmetic  25.8 us (4%)
  between operations  16 us (3%)
    psum x2, waiting for transfers between devices, shards(): weight_grads = lax.psum(lax.psum(weight_grads, 'ctx'), 'dp')  213 us
    all_gather x2, waiting for transfers between devices, shards(): gathered = lax.all_gather(own_rows, 'ctx', axis=0, tiled=True)  114 us
    reduce_scatter x2, waiting for transfers between devices, shards(): lax.psum_scatter(jnp.concatenate([key_grad, value_grad], axis=1).astype(j...  108 us
    ppermute x2, starting transfers between devices, from_behind(): return lax.ppermute(block, axis, route)  28.1 us
    dynamic_update_slice x8, local copies, waits for them, and re-layouts, shards(): probs, attended = lax.map(forward_group, query_groups)  22.5 us
    dot_general x4, matrix products, shards(): jnp.einsum('hqk,qhd->kd', score_grad, query_groups[head_block], preferred...  15.3 us
  transfers between devices with their start and end apart: 8, of which 8 were waited for; matrix products, arithmetic and copies ran while one was open for 12% of the time, Pallas kernels for 0%

profile of v1, /device:TPU:1, one launch (start us, length us, event | category | flops | bytes accessed | tf_op | source)
XLA Modules:
  0.0 602.1 jit_solution(10659373649664996307)
XLA Ops:
  16.2 65.9 %all-gather.3.cloned.1.call-done = bf16[2048,256]{1,0:T(8,128)(2,1)} async-done(((bf16[128,256]{1,0:T(8,128)(2,1)}), bf16[2048,256]{1,0:T(8,128)(2,1)}) %all-gather.3.cloned.1.call-update) | async-done | bytes 1048592 | tf_op jit(solution)/shard_map/all_gather | solution.py:65
  84.2 2.5 broadcast.232.clone2
  86.7 22.0 %while.26 = (s32[]{:T(128)}, bf16[2,4,128,2048]{2,3,1,0:T(8,128)(2,1)}, f32[2,128,4,128]{3,1,2,0:T(8,128)}, bf16[2,128,4,128]{1,3,2,0:T(8,128)(2,1)}, bf16[2048,...) while((s32[]{:T(128)}, ...), condition=%wide.region_7.8_spmd.clone, body=%wide.region_5.7_spmd.clone.sunk | while | flops 548666880 | bytes 33962720 | solution.py:85
  86.9 2.3 bitcast_reduce_fusion.4
  92.0 2.5 copy.225
  94.5 3.2 constant_dynamic-update-slice_fusion.4
  97.9 2.3 bitcast_reduce_fusion.4
  103.0 2.5 copy.225
  105.5 3.1 constant_dynamic-update-slice_fusion.4
  111.6 14.1 %collective-permute-start = (bf16[128,1024]{1,0:T(8,128)(2,1)S(1)}, bf16[128,1024]{1,0:T(8,128)(2,1)S(1)}, u32[]{:S(2)}, u32[]{:S(2)}) collective-permute-start(bf16[128,1024]{1,0:T(8,128)(2,1)S(1)} %fusion.63), channel_id=1, source_target_pairs={{448,0},{0,64},{64,128},{128,192},{192,256},{256,320},{320,384},{3... | collective-permute-start | bytes 786440 | tf_op jit(solution)/shard_map/ppermute | solution.py:13
  126.5 2.7 collective-permute-done
  136.3 2.3 fusion.38
  138.6 4.0 convolution_bitcast_fusion.8
  142.6 3.4 fusion.39
  148.6 48.4 %all-gather.5.cloned.1.call-done = bf16[2048,256]{1,0:T(8,128)(2,1)} async-done(((bf16[128,256]{1,0:T(8,128)(2,1)}), bf16[2048,256]{1,0:T(8,128)(2,1)}) %all-gather.5.cloned.1.call-update) | async-done | bytes 1048592 | tf_op jit(solution)/shard_map/all_gather | solution.py:65
  199.2 2.5 broadcast.232.clone
  201.6 21.9 %while.27 = (s32[]{:T(128)}, bf16[2,4,128,2048]{2,3,1,0:T(8,128)(2,1)}, f32[2,128,4,128]{3,1,2,0:T(8,128)}, bf16[2,128,4,128]{1,3,2,0:T(8,128)(2,1)}, bf16[2048,...) while((s32[]{:T(128)}, ...), condition=%wide.region_15.16_spmd.clone, body=%wide.region_13.15_spmd.clone.sunk | while | flops 548666880 | bytes 33962720 | solution.py:85
  201.9 2.3 bitcast_reduce_fusion.5
  207.0 2.5 copy.226
  209.5 3.2 constant_dynamic-update-slice_fusion.5
  212.9 2.3 bitcast_reduce_fusion.5
  218.0 2.5 copy.226
  220.5 3.1 constant_dynamic-update-slice_fusion.5
  229.7 3.9 convolution_bitcast_fusion.4
  233.6 4.0 fusion.37
  239.9 34.3 %reduce-scatter.3.cloned.1.call-done = bf16[128,256]{1,0:T(8,128)(2,1)} async-done(((bf16[2048,256]{1,0:T(8,128)(2,1)}), bf16[128,256]{1,0:T(8,128)(2,1)}) %reduce-scatter.3.cloned.1.call-update) | async-done | bytes 65552 | tf_op jit(solution)/shard_map/reduce_scatter | solution.py:123
  277.1 73.9 %reduce-scatter.5.cloned.1.call-done = bf16[128,256]{1,0:T(8,128)(2,1)} async-done(((bf16[2048,256]{1,0:T(8,128)(2,1)}), bf16[128,256]{1,0:T(8,128)(2,1)}) %reduce-scatter.5.cloned.1.call-update) | async-done | bytes 65552 | tf_op jit(solution)/shard_map/reduce_scatter | solution.py:123
  355.8 157.4 %all-reduce.3.cloned.1.call-done = f32[2,1024,256]{2,1,0:T(8,128)} async-done(((f32[2,1024,256]{2,1,0:T(8,128)}), f32[2,1024,256]{2,1,0:T(8,128)}) %all-reduce.3.cloned.1.call-update) | async-done | bytes 2097168 | tf_op jit(solution)/shard_map/psum | solution.py:142
  516.1 14.0 %collective-permute-start.1 = (bf16[128,1024]{1,0:T(8,128)(2,1)S(1)}, bf16[128,1024]{1,0:T(8,128)(2,1)S(1)}, u32[]{:S(2)}, u32[]{:S(2)}) collective-permute-start(bf16[128,1024]{1,0:T(8,128)(2,1)S(1)} %add_convert_fusion), channel_id=1, source_target_pairs={{448,0},{0,64},{64,128},{128,192},{192,256},{256,320},{320,384},{3... | collective-permute-start | bytes 786440 | tf_op jit(solution)/shard_map/ppermute | solution.py:13
  530.1 5.7 collective-permute-done.1
  535.8 55.7 %all-reduce.5.cloned.1.call-done = f32[2,1,1024,256]{3,2,1,0:T(8,128)} async-done(((f32[2,1,1024,256]{3,2,1,0:T(8,128)}), f32[2,1,1024,256]{3,2,1,0:T(8,128)}) %all-reduce.5.cloned.1.call-update) | async-done | bytes 2097168 | tf_op jit(solution)/shard_map/psum | solution.py:142
  592.2 3.0 copy.257
  (163 shorter events, 56.4 us)
Async XLA Ops:
  7.2 3.3 copy-start
  7.2 8.0 %copy-start.23 = (s32[32]{0:T(128)S(1)}, s32[32]{0:T(128)}, u32[]{:S(2)}) copy-start(s32[32]{0:T(128)} %param.13) | copy-start | bytes 388
  7.2 74.9 %all-gather.3.cloned.1.call-start = ((), (), s32[]{:S(2)}) async-start(), calls=%async_computation.2 | async-start | bytes 1114112 | tf_op jit(solution)/shard_map/all_gather | solution.py:65
  12.6 184.4 %all-gather.5.cloned.1.call-start = ((), (), s32[]{:S(2)}) async-start(), calls=%async_computation.3 | async-start | bytes 1114112 | tf_op jit(solution)/shard_map/all_gather | solution.py:65
  86.7 24.8 %copy-start.1 = (bf16[1,1,128,1024]{3,2,1,0:T(8,128)(2,1)S(1)}, bf16[1,1,128,1024]{3,2,1,0:T(8,128)(2,1)}, u32[]{:S(2)}) copy-start(bf16[1,1,128,1024]{3,2,1,0:T(8,128)(2,1)} %param.9) | copy-start | bytes 786436
  94.5 3.2 copy-start.14
  94.5 3.2 copy-start.16
  97.7 2.6 copy-start.15
  105.5 3.1 copy-start.14
  105.5 3.1 copy-start.16
  108.6 22.1 %copy-start.8 = (bf16[2,1,1,128,1024]{4,3,2,1,0:T(8,128)(2,1)S(1)}, bf16[2,1,1,128,1024]{4,3,2,1,0:T(8,128)(2,1)}, u32[]{:S(2)}) copy-start(bf16[2,1,1,128,1024]{4,3,2,1,0:T(8,128)(2,1)} %param.11) | copy-start | bytes 1572868
  111.6 17.5 %collective-permute-start = (bf16[128,1024]{1,0:T(8,128)(2,1)S(1)}, bf16[128,1024]{1,0:T(8,128)(2,1)S(1)}, u32[]{:S(2)}, u32[]{:S(2)}) collective-permute-start(bf16[128,1024]{1,0:T(8,128)(2,1)S(1)} %fusion.63), channel_id=1, source_target_pairs={{448,0},{0,64},{64,128},{128,192},{192,256},{256,320},{320,384},{3... | collective-permute-start | bytes 786440 | tf_op jit(solution)/shard_map/ppermute | solution.py:13
  129.1 18.6 %copy-start.2 = (bf16[128,1024]{1,0:T(8,128)(2,1)}, bf16[128,1024]{1,0:T(8,128)(2,1)S(1)}, u32[]{:S(2)}) copy-start(bf16[128,1024]{1,0:T(8,128)(2,1)S(1)} %collective-permute-done) | copy-start | bytes 786436
  129.6 4.4 copy-start.5
  130.6 143.5 %reduce-scatter.3.cloned.1.call-start = ((), (), s32[]{:S(2)}) async-start(), calls=%async_computation.4 | async-start | bytes 1114112 | tf_op jit(solution)/shard_map/reduce_scatter | solution.py:123
  147.1 203.9 %reduce-scatter.5.cloned.1.call-start = ((), (), s32[]{:S(2)}) async-start(), calls=%async_computation.5 | async-start | bytes 1114112 | tf_op jit(solution)/shard_map/reduce_scatter | solution.py:123
  209.5 3.2 copy-start.10
  209.5 3.2 copy-start.12
  212.6 2.6 copy-start.9
  212.6 2.6 copy-start.11
  220.5 3.1 copy-start.10
  220.5 3.1 copy-start.12
  223.6 3.8 copy-start.4
  223.6 6.1 %copy-start.7 = (bf16[2048,256]{1,0:T(8,128)(2,1)S(1)}, bf16[2048,256]{1,0:T(8,128)(2,1)}, u32[]{:S(2)}) copy-start(bf16[2048,256]{1,0:T(8,128)(2,1)} %all-gather.5.cloned.1.call-done) | copy-start | bytes 3145732
  233.6 43.1 %copy-start.20 = (f32[128]{0:T(128)S(1)}, f32[128]{0:T(128)}, u32[]{:S(2)}) copy-start(f32[128]{0:T(128)} %copy-done.19) | copy-start | bytes 1540
  237.6 113.4 %copy-start.6 = (f32[128,256]{1,0:T(8,128)S(1)}, f32[128,256]{1,0:T(8,128)}, u32[]{:S(2)}) copy-start(f32[128,256]{1,0:T(8,128)} %copy-done.5) | copy-start | bytes 393220
  237.6 113.4 %copy-start.18 = (f32[128]{0:T(128)S(1)}, f32[128]{0:T(128)}, u32[]{:S(2)}) copy-start(f32[128]{0:T(128)} %copy-done.17) | copy-start | bytes 1540
  237.6 116.0 %copy-start.3 = (bf16[128,1024]{1,0:T(8,128)(2,1)S(1)}, bf16[128,1024]{1,0:T(8,128)(2,1)}, u32[]{:S(2)}) copy-start(bf16[128,1024]{1,0:T(8,128)(2,1)} %copy-done.2) | copy-start | bytes 786436
  237.6 116.0 %copy-start.22 = (f32[128]{0:T(128)S(1)}, f32[128]{0:T(128)}, u32[]{:S(2)}) copy-start(f32[128]{0:T(128)} %copy-done.21) | copy-start | bytes 1540
  239.8 273.3 %all-reduce.3.cloned.1.call-start = ((), (), s32[]{:S(2)}) async-start(), calls=%async_computation.6 | async-start | bytes 4194304 | tf_op jit(solution)/shard_map/psum | solution.py:142
  355.7 235.8 %all-reduce.5.cloned.1.call-start = ((), (), s32[]{:S(2)}) async-start(), calls=%async_computation.7 | async-start | bytes 4194304 | tf_op jit(solution)/shard_map/psum | solution.py:142
  516.1 19.7 %collective-permute-start.1 = (bf16[128,1024]{1,0:T(8,128)(2,1)S(1)}, bf16[128,1024]{1,0:T(8,128)(2,1)S(1)}, u32[]{:S(2)}, u32[]{:S(2)}) collective-permute-start(bf16[128,1024]{1,0:T(8,128)(2,1)S(1)} %add_convert_fusion), channel_id=1, source_target_pairs={{448,0},{0,64},{64,128},{128,192},{192,256},{256,320},{320,384},{3... | collective-permute-start | bytes 786440 | tf_op jit(solution)/shard_map/ppermute | solution.py:13
  (8 other events, 15.7 us)
Sparse Core Ops, SparseCore 0:
  12.8 69.2 all-gather.2
  130.8 66.2 all-gather.4
  199.9 74.2 reduce-scatter.2
  277.6 73.3 reduce-scatter.4
  355.8 157.2 all-reduce.2
  515.4 76.0 all-reduce.4
